TPU v7x, 32 devices: a whole 2x2x4 slice. The times are simulated.
32 devices in a mesh: dp: 8 (over y, x, core), tensor: 4 (over z).
Axes of the slice: x: 2, y: 2, z: 4, core: 2. Of those that a mesh axis runs over, the one named last changes fastest.
Arguments:
- tokens: bfloat16 [32768, 768], P(('dp', 'tensor')), may hold values from -6 to 6
- qkv_weight: bfloat16 [768, 3, 768], P('dp', None, 'tensor'), may hold values from -0.3125 to 0.3125
- qv_bias: float32 [2, 768], replicated, may hold values from -3 to 3
- out_weight: bfloat16 [768, 768], P('dp', 'tensor'), may hold values from -0.875 to 0.875
- out_bias: float32 [768], replicated, may hold values from -2 to 2
- norm1_gain: float32 [768], replicated, may hold values from 0.1 to 1.9
- norm1_shift: float32 [768], replicated, may hold values from -2 to 2
- in_weight: bfloat16 [768, 2, 3072], P('dp', None, 'tensor'), may hold values from -0.21875 to 0.21875
- down_weight: bfloat16 [768, 3072], P('dp', 'tensor'), may hold values from -0.15625 to 0.15625
- down_bias: float32 [768], replicated, may hold values from -2 to 2
- norm2_gain: float32 [768], replicated, may hold values from 0.1 to 1.9
- norm2_shift: float32 [768], replicated, may hold values from -2 to 2
- cotangent: bfloat16 [32768, 768], P(('dp', 'tensor')), may hold values from -6 to 6
Outputs:
- layer_out: bfloat16 [32768, 768], P(('dp', 'tensor'))
- tokens_grad: bfloat16 [32768, 768], P(('dp', 'tensor'))
- qkv_weight_grad: float32 [768, 3, 768], P('dp', None, 'tensor')
- qv_bias_grad: float32 [2, 768], replicated
- out_weight_grad: float32 [768, 768], P('dp', 'tensor')
- out_bias_grad: float32 [768], replicated
- norm1_gain_grad: float32 [768], replicated
- norm1_shift_grad: float32 [768], replicated
- in_weight_grad: float32 [768, 2, 3072], P('dp', None, 'tensor')
- down_weight_grad: float32 [768, 3072], P('dp', 'tensor')
- down_bias_grad: float32 [768], replicated
- norm2_gain_grad: float32 [768], replicated
- norm2_shift_grad: float32 [768], replicated
All inputs are finite; a program needn't handle non-finite values.
Results may differ from a plain program's by a relative error of at most 0.02.
The roundings to bfloat16 on the way count: a program that leaves them out, or rounds other values in their place, can miss the bound.
Values may be sent and summed in bfloat16 or wider, within the bound.
No kernel may reach another device: no remote copies, remote signals or barrier semaphores. Data moves between devices by JAX's collectives and lax.ppermute only.
A program may use at most 192 MiB of HBM per device.

v0:
```python
import math
import jax
import jax.numpy as jnp
from jax import lax
from jax.sharding import PartitionSpec as P

HEAD = 64
SEQ = 1024
NORM_EPS = 1e-12
INV_ROOT_TWO = 0.7071067811865476
INV_ROOT_TWO_PI = 0.3989422804014327


def head_slopes(first_head, head_count):
    head_ids = first_head + jnp.arange(head_count, dtype=jnp.int32)
    powers = jnp.where(
        head_ids < 8, -(head_ids + 1).astype(jnp.float32), 7.5 - head_ids.astype(jnp.float32)
    )
    return jnp.exp2(powers)


def norm_forward(resid, gain, shift):
    center = resid - jnp.mean(resid, axis=1, keepdims=True)
    inverse = lax.rsqrt(jnp.mean(center * center, axis=1, keepdims=True) + NORM_EPS)
    normed = center * inverse
    return (normed * gain + shift, normed, inverse)


def norm_backward(grad_rows, normed, inverse, gain):
    scaled = grad_rows * gain
    first_mean = jnp.mean(scaled, axis=1, keepdims=True)
    second_mean = jnp.mean(scaled * normed, axis=1, keepdims=True)
    d_resid = inverse * (scaled - first_mean - normed * second_mean)
    return (d_resid, jnp.sum(grad_rows * normed, axis=0), jnp.sum(grad_rows, axis=0))


def make_scores(queries, key_rows, slope_value):
    length = queries.shape[0]
    position = jnp.arange(length, dtype=jnp.float32)
    distance = jnp.abs(position[:, None] - position[None, :])
    raw_scores = jnp.einsum("qd,kd->qk", queries, key_rows, preferred_element_type=jnp.float32)
    return raw_scores * (1.0 / math.sqrt(queries.shape[1])) - slope_value * distance


def attend_forward(item):
    queries, key_rows, value_rows, slope_value = item
    scores = make_scores(queries, key_rows, slope_value)
    row_max = jnp.max(scores, axis=1, keepdims=True)
    weights = jnp.exp(scores - row_max)
    row_sum = jnp.sum(weights, axis=1, keepdims=True)
    probs_low = (weights / row_sum).astype(jnp.bfloat16)
    context = jnp.dot(probs_low, value_rows, preferred_element_type=jnp.float32).astype(
        jnp.bfloat16
    )
    return (context, (row_max + jnp.log(row_sum))[:, 0])


def attend_backward(item):
    queries, key_rows, value_rows, log_total, d_context, slope_value = item
    scores = make_scores(queries, key_rows, slope_value)
    probs = jnp.exp(scores - log_total[:, None])
    probs_low = probs.astype(jnp.bfloat16)
    d_values = jnp.einsum("qk,qd->kd", probs_low, d_context, preferred_element_type=jnp.float32)
    d_probs = jnp.einsum("qd,kd->qk", d_context, value_rows, preferred_element_type=jnp.float32)
    inner_sum = jnp.sum(probs * d_probs, axis=1, keepdims=True)
    d_scores = (probs * (d_probs - inner_sum)).astype(jnp.bfloat16)
    scale_factor = 1.0 / math.sqrt(queries.shape[1])
    d_queries = jnp.dot(d_scores, key_rows, preferred_element_type=jnp.float32) * scale_factor
    d_keys = (
        jnp.einsum("qk,qd->kd", d_scores, queries, preferred_element_type=jnp.float32)
        * scale_factor
    )
    return (d_queries, d_keys, d_values)


def to_items(matrix, head_count):
    seq_count = matrix.shape[0] // SEQ
    each_width = matrix.shape[1] // head_count
    shaped = matrix.reshape(seq_count, SEQ, head_count, each_width).transpose(0, 2, 1, 3)
    return shaped.reshape(seq_count * head_count, SEQ, each_width)


def from_items(items, head_count):
    seq_count = items.shape[0] // head_count
    shaped = items.reshape(seq_count, head_count, SEQ, items.shape[2]).transpose(0, 2, 1, 3)
    return shaped.reshape(seq_count * SEQ, head_count * items.shape[2])


def fetch_weights(qkv_weight, in_weight, out_weight, down_weight):
    qkv_rows, in_rows, out_rows, down_rows = (
        lax.all_gather(qkv_weight, "dp", axis=0, tiled=True),
        lax.all_gather(in_weight, "dp", axis=0, tiled=True),
        lax.all_gather(out_weight, "dp", axis=0, tiled=True),
        lax.all_gather(down_weight, "dp", axis=0, tiled=True),
    )
    return (qkv_rows, in_rows, out_rows, down_rows)


def gelu_parts(gate_part):
    normal_cdf = 0.5 * (1.0 + lax.erf(gate_part * INV_ROOT_TWO))
    density = jnp.exp(-0.5 * gate_part * gate_part) * INV_ROOT_TWO_PI
    return (gate_part * normal_cdf, normal_cdf + gate_part * density)


def local(
    tokens,
    qkv_weight,
    qv_bias,
    out_weight,
    out_bias,
    norm1_gain,
    norm1_shift,
    in_weight,
    down_weight,
    down_bias,
    norm2_gain,
    norm2_shift,
    cotangent,
):
    model_width = tokens.shape[1]
    qkv_full, in_full, out_full, down_full = fetch_weights(
        qkv_weight, in_weight, out_weight, down_weight
    )
    local_width = qkv_full.shape[2]
    hidden_width = in_full.shape[2]
    head_count = local_width // HEAD
    col_start = lax.axis_index("tensor") * local_width
    group_rows = lax.all_gather(tokens, "tensor", axis=0, tiled=True)
    seq_count = group_rows.shape[0] // SEQ
    item_slopes = jnp.tile(head_slopes(col_start // HEAD, head_count), seq_count)
    bias_local = lax.dynamic_slice_in_dim(qv_bias, col_start, local_width, 1)
    projected = jnp.dot(
        group_rows,
        qkv_full.reshape(model_width, 3 * local_width),
        preferred_element_type=jnp.float32,
    )
    queries = (projected[:, :local_width] + bias_local[0]).astype(jnp.bfloat16)
    key_rows = projected[:, local_width : 2 * local_width].astype(jnp.bfloat16)
    value_rows = (projected[:, 2 * local_width :] + bias_local[1]).astype(jnp.bfloat16)
    query_items = to_items(queries, head_count)
    key_items = to_items(key_rows, head_count)
    value_items = to_items(value_rows, head_count)
    context_items, log_totals = lax.map(
        attend_forward, (query_items, key_items, value_items, item_slopes)
    )
    context = from_items(context_items, head_count)
    attn_partial = jnp.einsum("rc,oc->ro", context, out_full, preferred_element_type=jnp.float32)
    attention = lax.psum_scatter(attn_partial, "tensor", scatter_dimension=0, tiled=True)
    resid1 = tokens.astype(jnp.float32) + attention + out_bias
    hidden1, normed1, inverse1 = norm_forward(resid1, norm1_gain, norm1_shift)
    hidden1_low = hidden1.astype(jnp.bfloat16)
    group_hidden = lax.all_gather(hidden1_low, "tensor", axis=0, tiled=True)
    gate_up = jnp.dot(
        group_hidden,
        in_full.reshape(model_width, 2 * hidden_width),
        preferred_element_type=jnp.float32,
    )
    gate_part = gate_up[:, :hidden_width]
    up_part = gate_up[:, hidden_width:]
    activated, slope_gelu = gelu_parts(gate_part)
    gated = (activated * up_part).astype(jnp.bfloat16)
    ffn_partial = jnp.einsum("rf,of->ro", gated, down_full, preferred_element_type=jnp.float32)
    ffn_out = lax.psum_scatter(ffn_partial, "tensor", scatter_dimension=0, tiled=True)
    resid2 = hidden1 + ffn_out + down_bias
    result, normed2, inverse2 = norm_forward(resid2, norm2_gain, norm2_shift)
    d_resid2, norm2_gain_grad, norm2_shift_grad = norm_backward(
        cotangent.astype(jnp.float32), normed2, inverse2, norm2_gain
    )
    down_bias_grad = jnp.sum(d_resid2, axis=0)
    d_ffn_low = d_resid2.astype(jnp.bfloat16)
    group_d_ffn = lax.all_gather(d_ffn_low, "tensor", axis=0, tiled=True)
    qkv_full, in_full, out_full, down_full = fetch_weights(
        qkv_weight, in_weight, out_weight, down_weight
    )
    d_gated = jnp.dot(group_d_ffn, down_full, preferred_element_type=jnp.float32)
    down_grad = jnp.einsum("ro,rf->of", group_d_ffn, gated, preferred_element_type=jnp.float32)
    d_gate_up = jnp.concatenate(
        [d_gated * up_part * slope_gelu, d_gated * activated], axis=1
    ).astype(jnp.bfloat16)
    in_grad = jnp.einsum(
        "rd,rc->dc", group_hidden, d_gate_up, preferred_element_type=jnp.float32
    ).reshape(model_width, 2, hidden_width)
    d_group_hidden = jnp.einsum(
        "rc,dc->rd",
        d_gate_up,
        in_full.reshape(model_width, 2 * hidden_width),
        preferred_element_type=jnp.float32,
    )
    d_hidden_ffn = lax.psum_scatter(d_group_hidden, "tensor", scatter_dimension=0, tiled=True)
    d_hidden1 = d_resid2 + d_hidden_ffn
    d_resid1, norm1_gain_grad, norm1_shift_grad = norm_backward(
        d_hidden1, normed1, inverse1, norm1_gain
    )
    out_bias_grad = jnp.sum(d_resid1, axis=0)
    d_attn_low = d_resid1.astype(jnp.bfloat16)
    group_d_attn = lax.all_gather(d_attn_low, "tensor", axis=0, tiled=True)
    d_context = jnp.dot(group_d_attn, out_full, preferred_element_type=jnp.float32).astype(
        jnp.bfloat16
    )
    out_grad = jnp.einsum("ro,rc->oc", group_d_attn, context, preferred_element_type=jnp.float32)
    d_query_items, d_key_items, d_value_items = lax.map(
        attend_backward,
        (
            query_items,
            key_items,
            value_items,
            log_totals,
            to_items(d_context, head_count),
            item_slopes,
        ),
    )
    d_queries = from_items(d_query_items, head_count)
    d_keys = from_items(d_key_items, head_count)
    d_values = from_items(d_value_items, head_count)
    bias_local_grad = jnp.stack([jnp.sum(d_queries, axis=0), jnp.sum(d_values, axis=0)])
    qv_grad = lax.dynamic_update_slice(
        jnp.zeros((2, model_width), jnp.float32),
        bias_local_grad,
        (jnp.zeros((), jnp.int32), col_start),
    )
    d_projected = jnp.concatenate([d_queries, d_keys, d_values], axis=1).astype(jnp.bfloat16)
    qkv_grad = jnp.einsum(
        "rd,rc->dc", group_rows, d_projected, preferred_element_type=jnp.float32
    ).reshape(model_width, 3, local_width)
    d_group_rows = jnp.einsum(
        "rc,dc->rd",
        d_projected,
        qkv_full.reshape(model_width, 3 * local_width),
        preferred_element_type=jnp.float32,
    )
    d_tokens_attn = lax.psum_scatter(
        d_group_rows.astype(jnp.bfloat16), "tensor", scatter_dimension=0, tiled=True
    ).astype(jnp.float32)
    tokens_grad = (d_resid1 + d_tokens_attn).astype(jnp.bfloat16)
    qkv_grad, in_grad, out_grad, down_grad = (
        lax.psum_scatter(qkv_grad, "dp", scatter_dimension=0, tiled=True),
        lax.psum_scatter(in_grad, "dp", scatter_dimension=0, tiled=True),
        lax.psum_scatter(out_grad, "dp", scatter_dimension=0, tiled=True),
        lax.psum_scatter(down_grad, "dp", scatter_dimension=0, tiled=True),
    )
    (
        qv_grad,
        out_bias_grad,
        norm1_gain_grad,
        norm1_shift_grad,
        down_bias_grad,
        norm2_gain_grad,
        norm2_shift_grad,
    ) = lax.psum(
        (
            qv_grad,
            out_bias_grad,
            norm1_gain_grad,
            norm1_shift_grad,
            down_bias_grad,
            norm2_gain_grad,
            norm2_shift_grad,
        ),
        ("dp", "tensor"),
    )
    return (
        result.astype(jnp.bfloat16),
        tokens_grad,
        qkv_grad,
        qv_grad,
        out_grad,
        out_bias_grad,
        norm1_gain_grad,
        norm1_shift_grad,
        in_grad,
        down_grad,
        down_bias_grad,
        norm2_gain_grad,
        norm2_shift_grad,
    )


def solution(mesh):
    placed = (
        P(("dp", "tensor"), None),
        P("dp", None, "tensor"),
        P(),
        P("dp", "tensor"),
        P(),
        P(),
        P(),
        P("dp", None, "tensor"),
        P("dp", "tensor"),
        P(),
        P(),
        P(),
        P(("dp", "tensor"), None),
    )
    return jax.shard_map(
        local,
        mesh=mesh,
        in_specs=placed,
        out_specs=(
            P(("dp", "tensor"), None),
            P(("dp", "tensor"), None),
            P("dp", None, "tensor"),
            P(),
            P("dp", "tensor"),
            P(),
            P(),
            P(),
            P("dp", None, "tensor"),
            P("dp", "tensor"),
            P(),
            P(),
            P(),
        ),
        check_vma=False,
    )
```

profile of v0, /device:TPU:0, one launch (start us, length us, event | category | flops | bytes accessed | tf_op | source)
XLA Modules:
  0.0 1840.1 jit_solution(1177063377857514128)
XLA Ops:
  10.0 14.6 all_gather.29
  25.5 8.5 all_gather.30
  34.9 93.6 %all-gather.7.cloned.1.call-done = bf16[4096,768]{1,0:T(8,128)(2,1)} async-done(((bf16[1024,768]{1,0:T(8,128)(2,1)}), bf16[4096,768]{1,0:T(8,128)(2,1)}) %all-gather.7.cloned.1.call-update) | async-done | bytes 6291472 | tf_op jit(solution)/shard_map/all_gather | solution.py:128
  128.5 6.0 fusion.74
  147.3 4.5 copy.45
  160.1 131.6 %while.26 = (s32[]{:T(128)}, bf16[12,1024,64]{1,2,0:T(8,128)(2,1)}, f32[12,1024]{1,0:T(8,128)}, bf16[12,1024,64]{2,1,0:T(8,128)(2,1)S(1)}, bf16[12,1024,64]{2,1,...) while((s32[]{:T(128)}, bf16[12,1024,64]{1,2,0:T(8,128)(2,1)}, ...), condition=%wide.region_3.4_spmd, body=%wide.region_0.3_spmd.sunk | while | flops 280034304 | bytes 30321288 | solution.py:143
  297.2 6.4 fusion.75
  304.5 209.3 %reduce-scatter.8.cloned.1.call-done = f32[1024,768]{1,0:T(8,128)} async-done(((f32[4096,768]{1,0:T(8,128)}), f32[1024,768]{1,0:T(8,128)}) %reduce-scatter.8.cloned.1.call-update) | async-done | bytes 3145744 | tf_op jit(solution)/shard_map/reduce_scatter | solution.py:148
  523.5 112.0 %all-gather.9.cloned.1.call-done = bf16[4096,768]{1,0:T(8,128)(2,1)} async-done(((bf16[1024,768]{1,0:T(8,128)(2,1)}), bf16[4096,768]{1,0:T(8,128)(2,1)}) %all-gather.9.cloned.1.call-update) | async-done | bytes 6291472 | tf_op jit(solution)/shard_map/all_gather | solution.py:152
  635.5 17.3 fusion.76
  652.8 12.2 multiply_convert_fusion.2
  665.0 10.4 fusion.77
  675.4 10.0 all-gather.15.cloned.1.call-start
  685.4 200.3 %reduce-scatter.10.cloned.1.call-done = f32[1024,768]{1,0:T(8,128)} async-done(((f32[4096,768]{1,0:T(8,128)}), f32[1024,768]{1,0:T(8,128)}) %reduce-scatter.10.cloned.1.call-update) | async-done | bytes 3145744 | tf_op jit(solution)/shard_map/reduce_scatter | solution.py:163
  898.2 116.5 %all-gather.15.cloned.1.call-done = bf16[4096,768]{1,0:T(8,128)(2,1)} async-done(((bf16[1024,768]{1,0:T(8,128)(2,1)}), bf16[4096,768]{1,0:T(8,128)(2,1)}) %all-gather.15.cloned.1.call-update) | async-done | bytes 6291472 | tf_op jit(solution)/shard_map/all_gather | solution.py:171
  1014.7 22.1 %fusion.50 = (bf16[4096,768]{0,1:T(8,128)(2,1)}, bf16[4096,768]{0,1:T(8,128)(2,1)}) fusion(f32[4096,1536]{0,1:T(8,128)} %fusion.76, bf16[4096,768]{1,0:T(8,128)(2,1)} %all-gather.15.cloned.1.call-done, bf16[768,768]{1,0:T(8,128)(2,1)} %all-gather.13.cloned.1.call-done), kind=kOutput, calls=%fused_computation.57 | convolution fusion | flops 4875878400 | bytes 45219840 | tf_op jit(solution)/shard_map/dot_general | solution.py:175
  1036.9 16.1 fusion.52
  1053.1 210.0 %reduce-scatter.12.cloned.1.call-done = f32[1024,768]{1,0:T(8,128)} async-done(((f32[4096,768]{1,0:T(8,128)}), f32[1024,768]{1,0:T(8,128)}) %reduce-scatter.12.cloned.1.call-update) | async-done | bytes 3145744 | tf_op jit(solution)/shard_map/reduce_scatter | solution.py:189
  1272.7 16.5 fusion.51
  1289.3 6.7 reshape.200
  1296.0 92.8 %all-gather.17.cloned.1.call-done = bf16[4096,768]{1,0:T(8,128)(2,1)} async-done(((bf16[1024,768]{1,0:T(8,128)(2,1)}), bf16[4096,768]{1,0:T(8,128)(2,1)}) %all-gather.17.cloned.1.call-update) | async-done | bytes 6291472 | tf_op jit(solution)/shard_map/all_gather | solution.py:196
  1388.8 6.2 convolution_convert_fusion.1
  1403.3 167.5 %while.27 = (s32[]{:T(128)}, f32[12,1024,64]{1,2,0:T(8,128)S(1)}, bf16[12,1024,64]{1,2,0:T(8,128)(2,1)}, f32[12,1024,64]{1,2,0:T(8,128)}, bf16[12,1024,64]{2,1,0...) while((s32[]{:T(128)}, f32[12,1024,64]{1,2,0:T(8,128)S(1)}, ...), condition=%wide.region_17.18_spmd, body=%wide.region_15.17_spmd.sunk | while | flops 683801600 | bytes 34104956 | solution.py:201
  1582.4 7.0 convolution_convert_fusion
  1589.5 10.5 fusion.80
  1600.1 5.5 fusion.79
  1605.7 7.6 fusion.78
  1627.3 47.4 %all-reduce.1 = (f32[2,768]{1,0:T(2,128)}, f32[768]{0:T(1024)}, f32[768]{0:T(1024)}, f32[768]{0:T(1024)}, f32[768]{0:T(1024)}, /*index=5*/f32[768]{0:T(1024)}, f32[768]{0:T(1024)}) all-reduce(f32[2,768]{1,0:T(2,128)S(1)} %dynamic_update_slice.21, f32[768]{0:T(1024)S(1)} %copy-done.23, ...), channel_id=1, replica_groups=mesh['dp'=8,'tensor'=4] {'dp','tensor'}, use_global_device_ids=true, to_apply=%region_22.23 | all-reduce | flops 6144 | bytes 49152 | tf_op jit(solution)/shard_map/psum | solution.py:249
  1674.8 24.9 %reduce-scatter.14.cloned.1.call-done = bf16[1024,768]{1,0:T(8,128)(2,1)} async-done(((bf16[4096,768]{1,0:T(8,128)(2,1)}), bf16[1024,768]{1,0:T(8,128)(2,1)}) %reduce-scatter.14.cloned.1.call-update) | async-done | bytes 1572880 | tf_op jit(solution)/shard_map/reduce_scatter | solution.py:231
  1702.5 44.0 %reduce-scatter.20.cloned.1.call-done = f32[96,768]{1,0:T(8,128)} async-done(((f32[768,768]{1,0:T(8,128)}), f32[96,768]{1,0:T(8,128)}) %reduce-scatter.20.cloned.1.call-update) | async-done | bytes 294928 | tf_op jit(solution)/shard_map/reduce_scatter | solution.py:239
  1746.5 39.0 %reduce-scatter.18.cloned.1.call-done = f32[96,192]{1,0:T(8,128)} async-done(((f32[768,192]{1,0:T(8,128)}), f32[96,192]{1,0:T(8,128)}) %reduce-scatter.18.cloned.1.call-update) | async-done | bytes 73744 | tf_op jit(solution)/shard_map/reduce_scatter | solution.py:238
  1785.5 46.8 %reduce-scatter.16.cloned.1.call-done = f32[96,3,192]{2,0,1:T(8,128)} async-done(((f32[768,3,192]{2,0,1:T(8,128)}), f32[96,3,192]{2,0,1:T(8,128)}) %reduce-scatter.16.cloned.1.call-update) | async-done | bytes 221200 | tf_op jit(solution)/shard_map/reduce_scatter | solution.py:236
  (345 shorter events, 397.5 us)
Async XLA Ops:
  8.0 17.5 copy-start.17
  8.0 120.5 %all-gather.7.cloned.1.call-start = ((), (), s32[]{:S(2)}) async-start(), calls=%async_computation.7 | async-start | bytes 7864320 | tf_op jit(solution)/shard_map/all_gather | solution.py:128
  8.8 505.1 %reduce-scatter.8.cloned.1.call-start = ((), (), s32[]{:S(2)}) async-start(), calls=%async_computation.8 | async-start | bytes 15728640 | tf_op jit(solution)/shard_map/reduce_scatter | solution.py:148
  25.5 109.0 %copy-start.13 = (bf16[768,3,192]{0,2,1:T(8,128)(2,1)}, bf16[768,3,192]{0,2,1:T(8,128)(2,1)S(1)}, u32[]{:S(2)}) copy-start(bf16[768,3,192]{0,2,1:T(8,128)(2,1)S(1)} %copy.42) | copy-start | bytes 2654212
  34.1 262.0 %copy-start.9 = (bf16[768,192]{1,0:T(8,128)(2,1)}, bf16[768,192]{1,0:T(8,128)(2,1)S(1)}, u32[]{:S(2)}) copy-start(bf16[768,192]{1,0:T(8,128)(2,1)S(1)} %all_gather.30) | copy-start | bytes 884740
  291.6 4.4 copy-start.7
  291.6 4.4 copy-start.29
  303.6 210.3 %copy-start.27 = (f32[768]{0:T(1024)S(1)}, f32[768]{0:T(1024)}, u32[]{:S(2)}) copy-start(f32[768]{0:T(1024)} %param.21) | copy-start | bytes 9220
  303.7 216.1 %all-gather.11.cloned.1.call-start = ((), (), s32[]{:S(2)}) async-start(), calls=%async_computation.10 | async-start | bytes 2654208 | tf_op jit(solution)/shard_map/all_gather | solution.py:92
  304.2 331.3 %all-gather.9.cloned.1.call-start = ((), (), s32[]{:S(2)}) async-start(), calls=%async_computation.9 | async-start | bytes 7864320 | tf_op jit(solution)/shard_map/all_gather | solution.py:152
  519.1 145.8 %all-gather.13.cloned.1.call-start = ((), (), s32[]{:S(2)}) async-start(), calls=%async_computation.11 | async-start | bytes 1327104 | tf_op jit(solution)/shard_map/all_gather | solution.py:94
  519.7 365.9 %reduce-scatter.10.cloned.1.call-start = ((), (), s32[]{:S(2)}) async-start(), calls=%async_computation.12 | async-start | bytes 15728640 | tf_op jit(solution)/shard_map/reduce_scatter | solution.py:163
  675.3 210.3 %copy-start.28 = (f32[768]{0:T(1024)S(1)}, f32[768]{0:T(1024)}, u32[]{:S(2)}) copy-start(f32[768]{0:T(1024)} %param.26) | copy-start | bytes 9220
  675.4 339.4 %all-gather.15.cloned.1.call-start = ((), (), s32[]{:S(2)}) async-start(), calls=%async_computation.13 | async-start | bytes 7864320 | tf_op jit(solution)/shard_map/all_gather | solution.py:171
  898.2 364.9 %reduce-scatter.12.cloned.1.call-start = ((), (), s32[]{:S(2)}) async-start(), calls=%async_computation.14 | async-start | bytes 15728640 | tf_op jit(solution)/shard_map/reduce_scatter | solution.py:189
  1014.7 22.1 %copy-start.11 = (bf16[96,8,2,768]{3,1,2,0:T(8,128)(2,1)S(1)}, bf16[96,8,2,768]{3,1,2,0:T(8,128)(2,1)}, u32[]{:S(2)}) copy-start(bf16[96,8,2,768]{3,1,2,0:T(8,128)(2,1)} %copy.53) | copy-start | bytes 7077892
  1053.0 335.8 %all-gather.17.cloned.1.call-start = ((), (), s32[]{:S(2)}) async-start(), calls=%async_computation.15 | async-start | bytes 7864320 | tf_op jit(solution)/shard_map/all_gather | solution.py:196
  1272.2 344.2 %all-reduce.4.cloned.1.call-start = ((), (), s32[]{:S(2)}) async-start(), calls=%async_computation.20 | async-start | bytes 9437184
  1295.9 92.9 %copy-start.10 = (bf16[768,192]{1,0:T(8,128)(2,1)S(1)}, bf16[768,192]{1,0:T(8,128)(2,1)}, u32[]{:S(2)}) copy-start(bf16[768,192]{1,0:T(8,128)(2,1)} %copy-done.9) | copy-start | bytes 884740
  1295.9 403.7 %reduce-scatter.14.cloned.1.call-start = ((), (), s32[]{:S(2)}) async-start(), calls=%async_computation.16 | async-start | bytes 7864320 | tf_op jit(solution)/shard_map/reduce_scatter | solution.py:231
  1398.8 4.5 copy-start.30
  1589.5 10.6 copy-start.6
  1589.5 157.0 %reduce-scatter.20.cloned.1.call-start = ((), (), s32[]{:S(2)}) async-start(), calls=%async_computation.19 | async-start | bytes 2654208 | tf_op jit(solution)/shard_map/reduce_scatter | solution.py:239
  1600.0 185.5 %reduce-scatter.18.cloned.1.call-start = ((), (), s32[]{:S(2)}) async-start(), calls=%async_computation.18 | async-start | bytes 884736 | tf_op jit(solution)/shard_map/reduce_scatter | solution.py:238
  1605.6 226.7 %reduce-scatter.16.cloned.1.call-start = ((), (), s32[]{:S(2)}) async-start(), calls=%async_computation.17 | async-start | bytes 2654208 | tf_op jit(solution)/shard_map/reduce_scatter | solution.py:236
  1618.4 8.8 copy-start.18
  1618.4 8.8 copy-start.19
  1618.4 8.9 copy-start.20
  1618.4 8.9 copy-start.23
  1618.4 8.9 copy-start.24
  1618.4 8.9 copy-start.25
  1618.5 81.2 %copy-start.3 = (f32[1024,768]{1,0:T(8,128)S(1)}, f32[1024,768]{1,0:T(8,128)}, u32[]{:S(2)}) copy-start(f32[1024,768]{1,0:T(8,128)} %copy-done.2) | copy-start | bytes 9437188
  (25 other events, 46.9 us)
Sparse Core Ops, SparseCore 0:
  10.4 118.0 all-gather.6
  303.8 210.0 reduce-scatter.7
  898.3 116.3 all-gather.14
  1272.4 116.3 all-gather.16
  1589.6 110.0 reduce-scatter.13
  1703.4 43.0 reduce-scatter.19
  1750.5 34.9 reduce-scatter.17
  1789.8 42.4 reduce-scatter.15
Sparse Core Ops, SparseCore 1:
  306.0 27.0 all-gather.10
  519.2 116.2 all-gather.8
  637.3 22.1 all-gather.12
  675.4 210.2 reduce-scatter.9
  1053.1 209.9 reduce-scatter.11
  1296.0 87.4 all-reduce.3
where the time goes:
time: 1850 us; the launch traced here: 1840 us
  waiting for transfers between devices  1190 us (64%)
  matrix products  346 us (19%)
  local copies, waits for them, and re-layouts  134 us (7%)
  blocking collectives  70.6 us (4%)
  other arithmetic  69.1 us (4%)
    reduce_scatter x1, waiting for transfers between devices, local(): lax.psum_scatter(d_group_hidden, 'tensor', scatter_dimension=0, tiled=True)  210 us
    reduce_scatter x1, waiting for transfers between devices, local(): lax.psum_scatter(attn_partial, 'tensor', scatter_dimension=0, tiled=True)  209 us
    reduce_scatter x1, waiting for transfers between devices, local(): lax.psum_scatter(ffn_partial, 'tensor', scatter_dimension=0, tiled=True)  200 us
    all_gather x1, waiting for transfers between devices, local(): group_d_ffn = lax.all_gather(d_ffn_low, 'tensor', axis=0, tiled=True)  116 us
    all_gather x1, waiting for transfers between devices, local(): group_hidden = lax.all_gather(hidden1_low, 'tensor', axis=0, tiled=True)  112 us
    all_gather x1, waiting for transfers between devices, local(): group_rows = lax.all_gather(tokens, 'tensor', axis=0, tiled=True)  93.6 us
    all_gather x1, waiting for transfers between devices, local(): group_d_attn = lax.all_gather(d_attn_low, 'tensor', axis=0, tiled=True)  92.8 us
    dot_general x24, matrix products, make_scores(): jnp.einsum('qd,kd->qk', queries, key_rows, preferred_element_type=jnp.flo...  73 us
  transfers between devices with their start and end apart: 14, of which 11 were waited for; matrix products, arithmetic and copies ran while one was open for 16% of the time, Pallas kernels for 0%

commit v1 on v0

--- a/solution.py
+++ b/solution.py
@@ -149,7 +149,14 @@
     resid1 = tokens.astype(jnp.float32) + attention + out_bias
     hidden1, normed1, inverse1 = norm_forward(resid1, norm1_gain, norm1_shift)
     hidden1_low = hidden1.astype(jnp.bfloat16)
-    group_hidden = lax.all_gather(hidden1_low, "tensor", axis=0, tiled=True)
+    ways, here = (lax.axis_size("tensor"), lax.axis_index("tensor"))
+    group_hidden, reach = (hidden1_low, 1)
+    while reach < ways:
+        theirs = lax.ppermute(group_hidden, "tensor", [(d, d ^ reach) for d in range(ways)])
+        mine_first = jnp.concatenate([group_hidden, theirs], axis=0)
+        theirs_first = jnp.concatenate([theirs, group_hidden], axis=0)
+        group_hidden = jnp.where(here & reach == 0, mine_first, theirs_first)
+        reach = 2 * reach
     gate_up = jnp.dot(
         group_hidden,
         in_full.reshape(model_width, 2 * hidden_width),

time: 1850 us -> 1920 us (1.038)
  waiting for transfers between devices: 1190 us -> 1240 us
    ppermute x0 -> x2, waiting for transfers between devices: none -> 166 us  [local(): lax.ppermute(group_hidden, 'tensor', [(d, d ^ reach) for d in range(ways)])]
    all_gather x1 -> x0, waiting for transfers between devices: 112 us -> none  [local(): group_hidden = lax.all_gather(hidden1_low, 'tensor', axis=0, tiled=True)]
  transfers between devices with their start and end apart: 14 -> 15, of which waited for: 11 -> 12; matrix products, arithmetic and copies ran while one was open for 16% -> 16% of each run, Pallas kernels for 0% -> 0%
where the time goes in v1:
time: 1920 us; the launch traced here: 1910 us
  waiting for transfers between devices  1240 us (65%)
  matrix products  352 us (18%)
  local copies, waits for them, and re-layouts  134 us (7%)
  other arithmetic  72.4 us (4%)
  blocking collectives  70.7 us (4%)
    reduce_scatter x1, waiting for transfers between devices, local(): lax.psum_scatter(d_group_hidden, 'tensor', scatter_dimension=0, tiled=True)  210 us
    reduce_scatter x1, waiting for transfers between devices, local(): lax.psum_scatter(attn_partial, 'tensor', scatter_dimension=0, tiled=True)  210 us
    reduce_scatter x1, waiting for transfers between devices, local(): lax.psum_scatter(ffn_partial, 'tensor', scatter_dimension=0, tiled=True)  202 us
    ppermute x2, waiting for transfers between devices, local(): lax.ppermute(group_hidden, 'tensor', [(d, d ^ reach) for d in range(ways)])  166 us
    all_gather x1, waiting for transfers between devices, local(): group_d_ffn = lax.all_gather(d_ffn_low, 'tensor', axis=0, tiled=True)  117 us
    all_gather x1, waiting for transfers between devices, local(): group_rows = lax.all_gather(tokens, 'tensor', axis=0, tiled=True)  93.6 us
    all_gather x1, waiting for transfers between devices, local(): group_d_attn = lax.all_gather(d_attn_low, 'tensor', axis=0, tiled=True)  88.9 us
    dot_general x24, matrix products, make_scores(): jnp.einsum('qd,kd->qk', queries, key_rows, preferred_element_type=jnp.flo...  73 us
  transfers between devices with their start and end apart: 15, of which 12 were waited for; matrix products, arithmetic and copies ran while one was open for 16% of the time, Pallas kernels for 0%

profile of v1, /device:TPU:0, one launch (start us, length us, event | category | flops | bytes accessed | tf_op | source)
XLA Modules:
  0.0 1906.8 jit_solution(17056025330861012192)
XLA Ops:
  10.0 14.6 all_gather.26
  25.5 8.5 all_gather.27
  34.9 93.6 %all-gather.6.cloned.1.call-done = bf16[4096,768]{1,0:T(8,128)(2,1)} async-done(((bf16[1024,768]{1,0:T(8,128)(2,1)}), bf16[4096,768]{1,0:T(8,128)(2,1)}) %all-gather.6.cloned.1.call-update) | async-done | bytes 6291472 | tf_op jit(solution)/shard_map/all_gather | solution.py:128
  128.5 6.0 fusion.76
  160.0 131.6 %while.26 = (s32[]{:T(128)}, bf16[12,1024,64]{1,2,0:T(8,128)(2,1)}, f32[12,1024]{1,0:T(8,128)}, bf16[12,1024,64]{2,1,0:T(8,128)(2,1)S(1)}, bf16[12,1024,64]{2,1,...) while((s32[]{:T(128)}, bf16[12,1024,64]{1,2,0:T(8,128)(2,1)}, ...), condition=%wide.region_3.4_spmd, body=%wide.region_0.3_spmd.sunk | while | flops 280034304 | bytes 30321288 | solution.py:143
  297.1 6.4 fusion.77
  303.9 209.9 %reduce-scatter.8.cloned.1.call-done = f32[1024,768]{1,0:T(8,128)} async-done(((f32[4096,768]{1,0:T(8,128)}), f32[1024,768]{1,0:T(8,128)}) %reduce-scatter.8.cloned.1.call-update) | async-done | bytes 3145744 | tf_op jit(solution)/shard_map/reduce_scatter | solution.py:148
  520.6 34.9 %collective-permute-done = bf16[1024,768]{1,0:T(8,128)(2,1)} collective-permute-done((bf16[1024,768]{1,0:T(8,128)(2,1)}, bf16[1024,768]{1,0:T(8,128)(2,1)}, u32[]{:S(2)}, u32[]{:S(2)}) %collective-permute-start) | collective-permute-done | bytes 1572896 | tf_op jit(solution)/shard_map/ppermute | solution.py:155
  567.3 131.2 %collective-permute-done.1 = bf16[2048,768]{1,0:T(8,128)(2,1)} collective-permute-done((bf16[2048,768]{1,0:T(8,128)(2,1)}, bf16[2048,768]{1,0:T(8,128)(2,1)}, u32[]{:S(2)}, u32[]{:S(2)}) %collective-permute-start.1) | collective-permute-done | bytes 3145760 | tf_op jit(solution)/shard_map/ppermute | solution.py:155
  698.5 20.0 %fusion.63 = f32[4096,1536]{0,1:T(8,128)} fusion(bf16[768,1536]{1,0:T(8,128)(2,1)} %bitcast.195, bf16[2048,768]{1,0:T(8,128)(2,1)} %collective-permute-done.1, bf16[2048,768]{1,0:T(8,128)(2,1)} %maximum_select_fusion.1, pred[]{:T(512)S(6)} %eq.6), kind=kOutput, calls=%fused_computation.102 | convolution fusion | flops 9691987968 | bytes 33816576 | tf_op jit(solution)/shard_map/dot_general | solution.py:160
  718.5 12.1 multiply_convert_fusion.2
  730.7 10.3 fusion.78
  741.0 10.0 all-gather.12.cloned.1.call-start
  751.1 202.1 %reduce-scatter.10.cloned.1.call-done = f32[1024,768]{1,0:T(8,128)} async-done(((f32[4096,768]{1,0:T(8,128)}), f32[1024,768]{1,0:T(8,128)}) %reduce-scatter.10.cloned.1.call-update) | async-done | bytes 3145744 | tf_op jit(solution)/shard_map/reduce_scatter | solution.py:170
  965.8 116.5 %all-gather.12.cloned.1.call-done = bf16[4096,768]{1,0:T(8,128)(2,1)} async-done(((bf16[1024,768]{1,0:T(8,128)(2,1)}), bf16[4096,768]{1,0:T(8,128)(2,1)}) %all-gather.12.cloned.1.call-update) | async-done | bytes 6291472 | tf_op jit(solution)/shard_map/all_gather | solution.py:178
  1082.3 22.1 %fusion.50 = (bf16[4096,768]{0,1:T(8,128)(2,1)}, bf16[4096,768]{0,1:T(8,128)(2,1)}) fusion(f32[4096,1536]{0,1:T(8,128)} %fusion.63, bf16[4096,768]{1,0:T(8,128)(2,1)} %all-gather.12.cloned.1.call-done, bf16[768,768]{1,0:T(8,128)(2,1)} %all-gather.10.cloned.1.call-done), kind=kOutput, calls=%fused_computation.57 | convolution fusion | flops 4875878400 | bytes 45219840 | tf_op jit(solution)/shard_map/dot_general | solution.py:182
  1104.3 16.1 fusion.52
  1120.5 210.2 %reduce-scatter.12.cloned.1.call-done = f32[1024,768]{1,0:T(8,128)} async-done(((f32[4096,768]{1,0:T(8,128)}), f32[1024,768]{1,0:T(8,128)}) %reduce-scatter.12.cloned.1.call-update) | async-done | bytes 3145744 | tf_op jit(solution)/shard_map/reduce_scatter | solution.py:196
  1339.2 20.4 %fusion.51 = f32[768,1536]{1,0:T(8,128)} fusion(bf16[4096,768]{0,1:T(8,128)(2,1)} %get-tuple-element.173, bf16[4096,768]{0,1:T(8,128)(2,1)} %get-tuple-element.172, bf16[2048,768]{1,0:T(8,128)(2,1)} %collective-permute-done.1, bf16[2048,768]{1,0:T(8,128)(2,1)} %maximum_select_fusion.1, pred[]{:T(512)S(6)} %eq.6), kind=kOutput, calls=%fused_computation.63 | convolution fusion | flops 9717153792 | bytes 23592960 | tf_op jit(solution)/shard_map/rd,rc->dc/dot_general | solution.py:187
  1359.6 6.7 reshape.200
  1366.4 88.9 %all-gather.14.cloned.1.call-done = bf16[4096,768]{1,0:T(8,128)(2,1)} async-done(((bf16[1024,768]{1,0:T(8,128)(2,1)}), bf16[4096,768]{1,0:T(8,128)(2,1)}) %all-gather.14.cloned.1.call-update) | async-done | bytes 6291472 | tf_op jit(solution)/shard_map/all_gather | solution.py:203
  1455.3 6.1 convolution_convert_fusion.1
  1469.8 167.6 %while.27 = (s32[]{:T(128)}, f32[12,1024,64]{1,2,0:T(8,128)S(1)}, bf16[12,1024,64]{1,2,0:T(8,128)(2,1)}, f32[12,1024,64]{1,2,0:T(8,128)}, bf16[12,1024,64]{2,1,0...) while((s32[]{:T(128)}, f32[12,1024,64]{1,2,0:T(8,128)S(1)}, ...), condition=%wide.region_17.18_spmd, body=%wide.region_15.17_spmd.sunk | while | flops 683801600 | bytes 34104956 | solution.py:208
  1649.0 7.0 convolution_convert_fusion
  1656.1 10.4 fusion.81
  1666.6 5.5 fusion.80
  1672.2 7.6 fusion.79
  1693.8 47.5 %all-reduce.1 = (f32[2,768]{1,0:T(2,128)}, f32[768]{0:T(1024)}, f32[768]{0:T(1024)}, f32[768]{0:T(1024)}, f32[768]{0:T(1024)}, /*index=5*/f32[768]{0:T(1024)}, f32[768]{0:T(1024)}) all-reduce(f32[2,768]{1,0:T(2,128)S(1)} %dynamic_update_slice.21, ...), channel_id=1, replica_groups=mesh['dp'=8,'tensor'=4] {'dp','tensor'}, use_global_device_ids=true, to_apply=%region_22.23 | all-reduce | flops 6144 | bytes 49152 | tf_op jit(solution)/shard_map/psum | solution.py:256
  1741.3 24.9 %reduce-scatter.14.cloned.1.call-done = bf16[1024,768]{1,0:T(8,128)(2,1)} async-done(((bf16[4096,768]{1,0:T(8,128)(2,1)}), bf16[1024,768]{1,0:T(8,128)(2,1)}) %reduce-scatter.14.cloned.1.call-update) | async-done | bytes 1572880 | tf_op jit(solution)/shard_map/reduce_scatter | solution.py:238
  1769.1 44.1 %reduce-scatter.20.cloned.1.call-done = f32[96,768]{1,0:T(8,128)} async-done(((f32[768,768]{1,0:T(8,128)}), f32[96,768]{1,0:T(8,128)}) %reduce-scatter.20.cloned.1.call-update) | async-done | bytes 294928 | tf_op jit(solution)/shard_map/reduce_scatter | solution.py:246
  1813.1 39.1 %reduce-scatter.18.cloned.1.call-done = f32[96,192]{1,0:T(8,128)} async-done(((f32[768,192]{1,0:T(8,128)}), f32[96,192]{1,0:T(8,128)}) %reduce-scatter.18.cloned.1.call-update) | async-done | bytes 73744 | tf_op jit(solution)/shard_map/reduce_scatter | solution.py:245
  1852.2 46.6 %reduce-scatter.16.cloned.1.call-done = f32[96,3,192]{2,0,1:T(8,128)} async-done(((f32[768,3,192]{2,0,1:T(8,128)}), f32[96,3,192]{2,0,1:T(8,128)}) %reduce-scatter.16.cloned.1.call-update) | async-done | bytes 221200 | tf_op jit(solution)/shard_map/reduce_scatter | solution.py:243
  (341 shorter events, 409.1 us)
Async XLA Ops:
  8.0 17.5 copy-start.17
  8.0 120.5 %all-gather.6.cloned.1.call-start = ((), (), s32[]{:S(2)}) async-start(), calls=%async_computation.7 | async-start | bytes 7864320 | tf_op jit(solution)/shard_map/all_gather | solution.py:128
  8.8 505.1 %reduce-scatter.8.cloned.1.call-start = ((), (), s32[]{:S(2)}) async-start(), calls=%async_computation.8 | async-start | bytes 15728640 | tf_op jit(solution)/shard_map/reduce_scatter | solution.py:148
  25.5 109.0 %copy-start.13 = (bf16[768,3,192]{0,2,1:T(8,128)(2,1)}, bf16[768,3,192]{0,2,1:T(8,128)(2,1)S(1)}, u32[]{:S(2)}) copy-start(bf16[768,3,192]{0,2,1:T(8,128)(2,1)S(1)} %copy.42) | copy-start | bytes 2654212
  34.1 261.9 %copy-start.9 = (bf16[768,192]{1,0:T(8,128)(2,1)}, bf16[768,192]{1,0:T(8,128)(2,1)S(1)}, u32[]{:S(2)}) copy-start(bf16[768,192]{1,0:T(8,128)(2,1)S(1)} %all_gather.27) | copy-start | bytes 884740
  291.6 4.4 copy-start.7
  291.6 4.4 copy-start.26
  303.6 210.3 %copy-start.24 = (f32[768]{0:T(1024)S(1)}, f32[768]{0:T(1024)}, u32[]{:S(2)}) copy-start(f32[768]{0:T(1024)} %param.21) | copy-start | bytes 9220
  303.6 260.0 %all-gather.8.cloned.1.call-start = ((), (), s32[]{:S(2)}) async-start(), calls=%async_computation.9 | async-start | bytes 2654208 | tf_op jit(solution)/shard_map/all_gather | solution.py:92
  519.1 36.5 %collective-permute-start = (bf16[1024,768]{1,0:T(8,128)(2,1)}, bf16[1024,768]{1,0:T(8,128)(2,1)}, u32[]{:S(2)}, u32[]{:S(2)}) collective-permute-start(bf16[1024,768]{1,0:T(8,128)(2,1)} %fusion.62), channel_id=1, source_target_pairs={{0,1},{1,0},{2,3},{3,2},{4,5},{5,4},{6,7},{7,6},{8,9},{9,8},{10,11... | collective-permute-start | bytes 4718600 | tf_op jit(solution)/shard_map/ppermute | solution.py:155
  520.6 210.1 %all-gather.10.cloned.1.call-start = ((), (), s32[]{:S(2)}) async-start(), calls=%async_computation.10 | async-start | bytes 1327104 | tf_op jit(solution)/shard_map/all_gather | solution.py:94
  560.0 138.5 %collective-permute-start.1 = (bf16[2048,768]{1,0:T(8,128)(2,1)}, bf16[2048,768]{1,0:T(8,128)(2,1)}, u32[]{:S(2)}, u32[]{:S(2)}) collective-permute-start(bf16[2048,768]{1,0:T(8,128)(2,1)} %maximum_select_fusion.1), channel_id=1, source_target_pairs={{0,2},{1,3},{2,0},{3,1},{4,6},{5,7},{6,4},{7,5},{8,10},{9,11},{10,... | collective-permute-start | bytes 9437192 | tf_op jit(solution)/shard_map/ppermute | solution.py:155
  563.5 389.7 %reduce-scatter.10.cloned.1.call-start = ((), (), s32[]{:S(2)}) async-start(), calls=%async_computation.11 | async-start | bytes 15728640 | tf_op jit(solution)/shard_map/reduce_scatter | solution.py:170
  741.0 212.2 %copy-start.25 = (f32[768]{0:T(1024)S(1)}, f32[768]{0:T(1024)}, u32[]{:S(2)}) copy-start(f32[768]{0:T(1024)} %param.26) | copy-start | bytes 9220
  741.0 341.2 %all-gather.12.cloned.1.call-start = ((), (), s32[]{:S(2)}) async-start(), calls=%async_computation.12 | async-start | bytes 7864320 | tf_op jit(solution)/shard_map/all_gather | solution.py:178
  956.7 3.2 copy-start.23
  965.7 365.0 %reduce-scatter.12.cloned.1.call-start = ((), (), s32[]{:S(2)}) async-start(), calls=%async_computation.13 | async-start | bytes 15728640 | tf_op jit(solution)/shard_map/reduce_scatter | solution.py:196
  1082.3 22.1 %copy-start.11 = (bf16[96,8,2,768]{3,1,2,0:T(8,128)(2,1)S(1)}, bf16[96,8,2,768]{3,1,2,0:T(8,128)(2,1)}, u32[]{:S(2)}) copy-start(bf16[96,8,2,768]{3,1,2,0:T(8,128)(2,1)} %copy.53) | copy-start | bytes 7077892
  1120.5 334.8 %all-gather.14.cloned.1.call-start = ((), (), s32[]{:S(2)}) async-start(), calls=%async_computation.14 | async-start | bytes 7864320 | tf_op jit(solution)/shard_map/all_gather | solution.py:203
  1338.7 344.3 %all-reduce.4.cloned.1.call-start = ((), (), s32[]{:S(2)}) async-start(), calls=%async_computation.19 | async-start | bytes 9437184
  1366.3 89.0 %copy-start.10 = (bf16[768,192]{1,0:T(8,128)(2,1)S(1)}, bf16[768,192]{1,0:T(8,128)(2,1)}, u32[]{:S(2)}) copy-start(bf16[768,192]{1,0:T(8,128)(2,1)} %copy-done.9) | copy-start | bytes 884740
  1366.4 399.8 %reduce-scatter.14.cloned.1.call-start = ((), (), s32[]{:S(2)}) async-start(), calls=%async_computation.15 | async-start | bytes 7864320 | tf_op jit(solution)/shard_map/reduce_scatter | solution.py:238
  1465.3 4.5 copy-start.27
  1637.4 2.7 copy-start.4
  1656.0 10.6 copy-start.6
  1656.0 157.1 %reduce-scatter.20.cloned.1.call-start = ((), (), s32[]{:S(2)}) async-start(), calls=%async_computation.18 | async-start | bytes 2654208 | tf_op jit(solution)/shard_map/reduce_scatter | solution.py:246
  1666.6 185.6 %reduce-scatter.18.cloned.1.call-start = ((), (), s32[]{:S(2)}) async-start(), calls=%async_computation.17 | async-start | bytes 884736 | tf_op jit(solution)/shard_map/reduce_scatter | solution.py:245
  1672.2 226.6 %reduce-scatter.16.cloned.1.call-start = ((), (), s32[]{:S(2)}) async-start(), calls=%async_computation.16 | async-start | bytes 2654208 | tf_op jit(solution)/shard_map/reduce_scatter | solution.py:243
  1685.0 8.8 copy-start.18
  1685.0 8.8 copy-start.21
  1685.0 8.8 copy-start.22
  1685.0 81.2 %copy-start.3 = (f32[1024,768]{1,0:T(8,128)S(1)}, f32[1024,768]{1,0:T(8,128)}, u32[]{:S(2)}) copy-start(f32[1024,768]{1,0:T(8,128)} %copy-done.2) | copy-start | bytes 9437188
  (23 other events, 41.0 us)
Sparse Core Ops, SparseCore 0:
  10.4 118.0 all-gather.5
  303.7 210.0 reduce-scatter.7
  741.2 211.9 reduce-scatter.9
  965.8 116.3 all-gather.11
  1120.6 210.0 reduce-scatter.11
  1338.9 116.4 all-gather.13
  1656.2 109.9 reduce-scatter.13
  1770.1 42.9 reduce-scatter.19
  1817.2 34.9 reduce-scatter.17
  1856.3 42.4 reduce-scatter.15
Sparse Core Ops, SparseCore 1:
  520.7 29.8 all-gather.7
  563.6 22.0 all-gather.9
  1366.4 87.4 all-reduce.3
